TPU v7x, 32 devices: a whole 2x2x4 slice. The times are simulated.
32 devices in a mesh: pb: 4 (over y, core), wa: 8 (over z, x).
Axes of the slice: x: 2, y: 2, z: 4, core: 2. Of those that a mesh axis runs over, the one named last changes fastest.
Arguments:
- state: float32 [2, 8388608], P(None, ('pb', 'wa')), may hold values from -6 to 6
- gate_bank: float32 [4, 2, 128, 128], replicated, may hold values from -0.375 to 0.375
- pass_order: int32 [4], replicated, may hold values from 0 to 3, each once
Outputs:
- evolved: float32 [2, 8388608], P(None, ('pb', 'wa'))
Inputs may be any that keep to these rules, and one draw needn't show every extreme that they name: `pass_order`: each pass index 0 to 3 appears once.
All inputs are finite; a program needn't handle non-finite values.
Results may differ from a plain program's by a relative error of at most 0.0001.
Values sent between devices are 32-bit elements; how exact they have to be, the bound alone decides.
A program may use at most 64 MiB of HBM per device.

v0:
```python
import jax
import jax.numpy as jnp
from jax import lax
from jax.sharding import PartitionSpec as P

HIGH = lax.Precision.HIGHEST


def mix_left(gate, values):
    real = jnp.dot(gate[0], values[0], precision=HIGH) - jnp.dot(gate[1], values[1], precision=HIGH)
    imag = jnp.dot(gate[0], values[1], precision=HIGH) + jnp.dot(gate[1], values[0], precision=HIGH)
    return jnp.stack([real, imag])


def mix_right(gate, values):
    real = jnp.dot(values[0], gate[0].T, precision=HIGH) - jnp.dot(
        values[1], gate[1].T, precision=HIGH
    )
    imag = jnp.dot(values[1], gate[0].T, precision=HIGH) + jnp.dot(
        values[0], gate[1].T, precision=HIGH
    )
    return jnp.stack([real, imag])


def select_gate(gate_bank, pass_order, which):
    picked = pass_order[which] == jnp.arange(gate_bank.shape[0], dtype=jnp.int32)
    return jnp.sum(jnp.where(picked[:, None, None, None], gate_bank, 0.0), axis=0)


def trade_global(packed):
    return lax.all_to_all(
        lax.all_to_all(packed, "pb", split_axis=1, concat_axis=1, tiled=True),
        "wa",
        split_axis=2,
        concat_axis=2,
        tiled=True,
    )


def pack_block(block, groups, wa_count, middle):
    shaped = block.reshape(2, groups, 2, middle, wa_count // 2, -1)
    moved = jnp.transpose(shaped, (0, 1, 2, 4, 3, 5))
    return moved.reshape(2, groups, wa_count, middle, -1)


def unpack_block(packed, groups, wa_count, middle):
    shaped = packed.reshape(2, groups, 2, wa_count // 2, middle, -1)
    return jnp.transpose(shaped, (0, 1, 2, 4, 3, 5)).reshape(2, -1)


def per_device(state, gate_bank, pass_order):
    groups = lax.axis_size("pb")
    wa_count = lax.axis_size("wa")
    gate_rows = gate_bank.shape[2]
    middle = gate_rows // (2 * groups)
    psi = state
    first = select_gate(gate_bank, pass_order, 0)
    psi = mix_right(first, psi.reshape(2, -1, gate_rows)).reshape(2, -1)
    packed = trade_global(pack_block(psi, groups, wa_count, middle))
    second = select_gate(gate_bank, pass_order, 1)
    shaped = packed.reshape(2, groups, 2, wa_count // 2, middle, -1)
    moved = jnp.transpose(shaped, (0, 1, 2, 4, 3, 5))
    moved_shape = moved.shape
    mixed = mix_left(second, moved.reshape(2, gate_rows, -1)).reshape(moved_shape)
    psi = jnp.transpose(mixed, (0, 1, 2, 4, 3, 5)).reshape(2, -1)
    third = select_gate(gate_bank, pass_order, 2)
    psi = mix_right(third, psi.reshape(2, -1, gate_rows)).reshape(2, -1)
    fourth = select_gate(gate_bank, pass_order, 3)
    shaped = psi.reshape(2, groups, wa_count // 2, 2, middle, -1)
    moved = jnp.transpose(shaped, (0, 1, 3, 4, 2, 5))
    moved_shape = moved.shape
    mixed = mix_left(fourth, moved.reshape(2, gate_rows, -1)).reshape(moved_shape)
    packed = jnp.transpose(mixed, (0, 1, 4, 2, 3, 5)).reshape(2, groups, wa_count, middle, -1)
    psi = unpack_block(trade_global(packed), groups, wa_count, middle)
    return psi


def solution(mesh):
    in_specs = (P(None, ("pb", "wa")), P(), P())
    out_specs = P(None, ("pb", "wa"))
    return jax.shard_map(
        per_device, mesh=mesh, in_specs=in_specs, out_specs=out_specs, check_vma=False
    )
```

profile of v0, /device:TPU:0, one launch (start us, length us, event | category | flops | bytes accessed | tf_op | source)
XLA Modules:
  0.0 210.9 jit_solution(14688105302782742132)
XLA Ops:
  0.0 1.5 fusion.14
  1.5 4.3 %fusion.13 = (f32[1,262144]{1,0:T(1,128)S(1)}, f32[1,262144]{1,0:T(1,128)S(1)}) fusion(f32[2,262144]{1,0:T(2,128)} %param.3), kind=kLoop, calls=%fused_computation.42 | loop fusion | bytes 4194304 | tf_op jit(solution)/shard_map/slice | solution.py:16
  5.7 1.3 iota_compare_fusion
  7.0 1.2 iota_compare_fusion.2
  8.2 0.2 select_reduce_fusion.3
  8.5 1.0 fusion.6
  9.5 1.0 fusion.7
  10.5 1.0 fusion
  11.6 1.0 fusion.1
  12.6 0.3 copy.25
  12.9 1.3 stack.36
  14.3 0.3 copy.26
  14.6 0.4 stack.37
  15.0 0.5 copy-done
  15.5 0.5 maximum_bitcast_fusion
  16.0 0.7 copy.41
  16.7 29.7 %all_to_all.20 = f32[2,4,8,16,512]{4,3,2,0,1:T(8,128)S(1)} all-to-all(f32[2,4,8,16,512]{4,3,2,0,1:T(8,128)S(1)} %bitcast.106), channel_id=1, replica_groups=mesh['pb'=4,'wa'=8] {'pb'}, dimensions={1} | all-to-all | bytes 4194304 | tf_op jit(solution)/shard_map/all_to_all | solution.py:32
  46.4 0.3 copy.29
  46.7 53.6 %all_to_all.21 = f32[2,4,8,16,512]{4,3,1,0,2:T(8,128)S(1)} all-to-all(f32[2,4,8,16,512]{4,3,1,0,2:T(8,128)S(1)} %copy.29), channel_id=1, replica_groups=mesh['pb'=4,'wa'=8] {'wa'}, dimensions={2} | all-to-all | bytes 4194304 | tf_op jit(solution)/shard_map/all_to_all | solution.py:31
  100.3 1.4 copy.48
  101.7 0.5 fusion.12
  102.2 0.3 copy.43
  102.5 0.3 copy.44
  102.9 1.0 fusion.4
  103.9 1.0 fusion.5
  104.9 1.0 convolution_add_fusion.2
  105.9 1.0 convolution_subtract_fusion.2
  106.9 0.7 stack.39
  107.7 1.3 copy.31
  108.9 0.7 stack.40
  109.7 0.3 copy.32
  110.0 0.2 copy-done.1
  110.2 0.2 maximum_bitcast_fusion.1
  110.4 0.2 fusion.11
  110.6 0.1 squeeze.88
  110.7 0.1 squeeze.91
  110.8 1.0 fusion.8
  111.8 1.0 fusion.9
  112.7 1.0 convolution_add_fusion.1
  113.7 1.2 convolution_subtract_fusion.1
  115.0 0.2 stack.42
  115.1 0.7 copy.33
  115.8 0.2 stack.43
  116.0 0.7 copy.34
  116.7 0.6 maximum_bitcast_fusion.2
  117.2 0.5 fusion.10
  117.7 0.3 copy.45
  118.1 0.3 copy.46
  118.4 1.0 fusion.2
  119.4 1.0 fusion.3
  120.4 1.0 convolution_add_fusion
  121.5 1.0 convolution_subtract_fusion
  122.5 0.7 stack.45
  123.2 1.3 copy.35
  124.5 0.7 stack.46
  125.2 0.3 copy.36
  125.5 0.2 copy-done.2
  125.7 0.2 pad_maximum_fusion
  126.0 0.3 copy.37
  126.3 28.1 %all_to_all.22 = f32[2,4,8,16,512]{4,3,2,0,1:T(8,128)S(1)} all-to-all(f32[2,4,8,16,512]{4,3,2,0,1:T(8,128)S(1)} %copy.37), channel_id=1, replica_groups=mesh['pb'=4,'wa'=8] {'pb'}, dimensions={1} | all-to-all | bytes 4194304 | tf_op jit(solution)/shard_map/all_to_all | solution.py:32
  154.4 0.3 copy.38
  154.7 51.3 %all_to_all.23 = f32[2,4,8,16,512]{4,3,1,0,2:T(8,128)S(1)} all-to-all(f32[2,4,8,16,512]{4,3,1,0,2:T(8,128)S(1)} %copy.38), channel_id=1, replica_groups=mesh['pb'=4,'wa'=8] {'wa'}, dimensions={2} | all-to-all | bytes 4194304 | tf_op jit(solution)/shard_map/all_to_all | solution.py:31
  206.0 1.4 copy.40
  207.4 3.5 %reshape.72 = f32[2,262144]{1,0:T(2,128)} reshape(f32[2,4,2,16,4,512]{5,4,3,2,1,0:T(4,128)S(1)} %copy.40) | data formatting | bytes 4194304 | tf_op jit(solution)/shard_map/reshape | solution.py:48
  (5 shorter events, 0.0 us)
Async XLA Ops:
  1.5 6.8 %copy-start.3 = (f32[4,2,128,128]{3,2,1,0:T(8,128)S(1)}, f32[4,2,128,128]{3,2,1,0:T(8,128)}, u32[]{:S(2)}) copy-start(f32[4,2,128,128]{3,2,1,0:T(8,128)} %param.4) | copy-start | bytes 1572868
  14.3 1.2 copy-start
  108.9 1.2 copy-start.1
  124.5 1.2 copy-start.2
where the time goes:
time: 211 us
  blocking collectives  163 us (77%)
  local copies, waits for them, and re-layouts  27.2 us (13%)
  matrix products  16.4 us (8%)
  other arithmetic  4.25 us (2%)
    all_to_all x2, blocking collectives, trade_global(): lax.all_to_all(lax.all_to_all(packed, 'pb', split_axis=1, concat_axis=1,...  105 us
    all_to_all x2, blocking collectives, trade_global(): lax.all_to_all(packed, 'pb', split_axis=1, concat_axis=1, tiled=True)  57.9 us
    another operation x8, local copies, waits for them, and re-layouts, mix_left(): return jnp.stack([real, imag])  6.06 us
    slice x2, local copies, waits for them, and re-layouts, mix_right(): values[0]  4.46 us

commit v1 on v0

v1 whole, which is shorter than its diff:
```python
import functools

import jax
import jax.numpy as jnp
from jax import lax
from jax.experimental import pallas as pl
from jax.experimental.pallas import tpu as pltpu
from jax.sharding import PartitionSpec as P

MESH = pl.DeviceIdType.MESH
HIGH = lax.Precision.HIGHEST
CHUNKS = 2
SUB = 8


def dot(a, b):
    return lax.dot_general(
        a, b, (((1,), (0,)), ((), ())), precision=HIGH, preferred_element_type=jnp.float32
    )


def dot_t(a, b):
    return lax.dot_general(
        a, b, (((1,), (1,)), ((), ())), precision=HIGH, preferred_element_type=jnp.float32
    )


def embed(real, imag):
    upper = jnp.concatenate([real, -imag], axis=1)
    lower = jnp.concatenate([imag, real], axis=1)
    return jnp.concatenate([upper, lower], axis=0)


def spread_rows(groups, mid, gate_rows, high):
    slot = lax.broadcasted_iota(jnp.int32, (2 * gate_rows, gate_rows), 0)
    row = lax.broadcasted_iota(jnp.int32, (2 * gate_rows, gate_rows), 1)
    a = row // (2 * mid)
    w0 = (row // mid) % 2
    m = row % mid
    return jnp.where(slot == ((w0 * groups + a) * 2 + high) * mid + m, 1.0, 0.0).astype(jnp.float32)


def kernel(groups, wa_count, mid, order_ref, bank_ref, x_ref, out_ref, lanes_gate, rows_gate,
           buf, obuf, fs, fr, bs, br, own):
    gate_rows = bank_ref.shape[2]
    rows = 2 * gate_rows
    a = lax.axis_index("pb")
    w = lax.axis_index("wa")
    half = wa_count // 2
    w2 = w // half
    w0 = w % 2
    wm = w - w2 * half - w0

    peers = []
    for dw2 in (1, 0):
        for da in range(groups):
            for dw0 in range(2):
                if dw2 or da or dw0:
                    peers.append(((a + da) % groups, (w2 + dw2) % 2, (w0 + dw0) % 2))

    def device(p):
        return (p[0], p[1] * half + wm + p[2])

    def slot(p):
        return (p[2] * groups + p[0]) * 2 + p[1]

    def piece(ref, p, c):
        return ref.at[p[0] * 2 + p[1], :, p[2], c]

    def held(ref, c, s):
        return ref.at[c, pl.ds(s * mid, mid)]

    me = (a, w2, w0)
    mine = slot(me)

    def forward(c, p):
        return pltpu.make_async_remote_copy(
            src_ref=piece(x_ref, p, c), dst_ref=held(buf, c, mine),
            send_sem=fs.at[c, slot(p)], recv_sem=fr.at[c, mine],
            device_id=device(p), device_id_type=MESH)

    def arriving(c, p):
        return pltpu.make_async_remote_copy(
            src_ref=piece(x_ref, p, c), dst_ref=held(buf, c, slot(p)),
            send_sem=fs.at[c, slot(p)], recv_sem=fr.at[c, slot(p)],
            device_id=device(p), device_id_type=MESH)

    def back(c, p):
        return pltpu.make_async_remote_copy(
            src_ref=held(obuf, c, slot(p)), dst_ref=piece(out_ref, me, c),
            send_sem=bs.at[c, slot(p)], recv_sem=br.at[c, mine],
            device_id=device(p), device_id_type=MESH)

    def returning(c, p):
        return pltpu.make_async_remote_copy(
            src_ref=held(obuf, c, slot(p)), dst_ref=piece(out_ref, p, c),
            send_sem=bs.at[c, slot(p)], recv_sem=br.at[c, slot(p)],
            device_id=device(p), device_id_type=MESH)

    barrier = pltpu.get_barrier_semaphore()
    for p in peers:
        pl.semaphore_signal(barrier, inc=1, device_id=device(p), device_id_type=MESH)
    pl.semaphore_wait(barrier, len(peers))

    for c in range(CHUNKS):
        for p in peers:
            forward(c, p).start()
    stay = [pltpu.make_async_copy(piece(x_ref, me, c), held(buf, c, mine), own.at[0, c])
            for c in range(CHUNKS)]
    for copy in stay:
        copy.start()

    gates = [bank_ref[order_ref[k]] for k in range(4)]
    first = embed(gates[0][0], gates[0][1])
    third = embed(gates[2][0], gates[2][1])
    lanes_gate[...] = dot(third, first)
    real, imag = 0.0, 0.0
    for high in range(2):
        spread = spread_rows(groups, mid, gate_rows, high)
        real += dot_t(dot(spread, gates[3][0]), spread)
        imag += dot_t(dot(spread, gates[3][1]), spread)
    zero = jnp.zeros((gate_rows, gate_rows), jnp.float32)
    halves = []
    for part in range(2):
        g = gates[1][part]
        halves.append(jnp.concatenate([
            jnp.concatenate([g, zero], axis=1), jnp.concatenate([zero, g], axis=1)], axis=0))
    both = dot(embed(real, imag), jnp.concatenate(halves, axis=0))
    rows_gate[:, :rows] = both
    rows_gate[:rows, rows:] = -both[rows:]
    rows_gate[rows:, rows:] = both[:rows]

    for c in range(CHUNKS):
        for p in peers:
            arriving(c, p).wait_recv()
        stay[c].wait()
        flat_in = buf.at[c].reshape(rows * SUB, buf.shape[-1])
        flat_out = obuf.at[c].reshape(rows * SUB, buf.shape[-1])
        for q in range(SUB // 2):
            re = flat_in[pl.ds(2 * q, rows, SUB), :]
            im = flat_in[pl.ds(2 * q + 1, rows, SUB), :]
            mixed = dot_t(jnp.concatenate([re, im], axis=1), lanes_gate[...])
            tall = jnp.concatenate([mixed[:, :gate_rows], mixed[:, gate_rows:]], axis=0)
            done = dot(rows_gate[...], tall)
            flat_out[pl.ds(2 * q, rows, SUB), :] = done[:rows]
            flat_out[pl.ds(2 * q + 1, rows, SUB), :] = done[rows:]
        for p in peers:
            back(c, p).start()
        pltpu.make_async_copy(held(obuf, c, mine), piece(out_ref, me, c), own.at[1, c]).start()

    for c in range(CHUNKS):
        for p in peers:
            returning(c, p).wait_recv()
        pltpu.make_async_copy(held(obuf, c, mine), piece(out_ref, me, c), own.at[1, c]).wait()
    for c in range(CHUNKS):
        for p in peers:
            forward(c, p).wait_send()
            back(c, p).wait_send()


def per_device(groups, wa_count, state, gate_bank, pass_order):
    lanes = gate_bank.shape[2]
    mid = lanes // (2 * groups)
    size = state.shape[1]
    shape = (2 * groups, mid, 2, CHUNKS, SUB, lanes)
    x = state.reshape(2, size // lanes, lanes).transpose(1, 0, 2).reshape(shape)
    slots = 4 * groups
    out = pl.pallas_call(
        functools.partial(kernel, groups, wa_count, mid),
        out_shape=jax.ShapeDtypeStruct(shape, jnp.float32),
        in_specs=[
            pl.BlockSpec(memory_space=pltpu.SMEM),
            pl.BlockSpec(memory_space=pltpu.VMEM),
            pl.BlockSpec(memory_space=pl.ANY),
        ],
        out_specs=pl.BlockSpec(memory_space=pl.ANY),
        scratch_shapes=[
            pltpu.VMEM((2 * lanes, 2 * lanes), jnp.float32),
            pltpu.VMEM((4 * lanes, 4 * lanes), jnp.float32),
            pltpu.VMEM((CHUNKS, 2 * lanes, SUB, lanes), jnp.float32),
            pltpu.VMEM((CHUNKS, 2 * lanes, SUB, lanes), jnp.float32),
            pltpu.SemaphoreType.DMA((CHUNKS, slots)),
            pltpu.SemaphoreType.DMA((CHUNKS, slots)),
            pltpu.SemaphoreType.DMA((CHUNKS, slots)),
            pltpu.SemaphoreType.DMA((CHUNKS, slots)),
            pltpu.SemaphoreType.DMA((2, CHUNKS)),
        ],
        compiler_params=pltpu.CompilerParams(collective_id=0, has_side_effects=True),
    )(pass_order, gate_bank, x)
    return out.reshape(size // lanes, 2, lanes).transpose(1, 0, 2).reshape(2, size)


def solution(mesh):
    in_specs = (P(None, ("pb", "wa")), P(), P())
    out_specs = P(None, ("pb", "wa"))
    return jax.shard_map(
        functools.partial(per_device, mesh.shape["pb"], mesh.shape["wa"]),
        mesh=mesh, in_specs=in_specs, out_specs=out_specs, check_vma=False,
    )
```

time: 211 us -> 102 us (0.48)
  blocking collectives: 163 us -> 0 us
  Pallas kernels: 0 us -> 99.6 us
  local copies, waits for them, and re-layouts: 27.2 us -> 2.61 us
  matrix products: 16.4 us -> 0 us
  other arithmetic: 4.25 us -> 0 us
    all_to_all x4 -> x0, blocking collectives: 163 us -> none  [the longest x2 105 us: trade_global(): lax.all_to_all(lax.all_to_all(packed, 'pb', split_axis=1, concat_axis=1,...]
    pallas_call x0 -> x1, Pallas kernels: none -> 99.6 us  [per_device(): pl.pallas_call(functools.partial(kernel, groups, wa_count, mid), out_shap...]
    dot_general x16 -> x0, matrix products: 16.4 us -> none  [the longest x2 2.23 us: mix_right(): jnp.dot(values[1], gate[1].T, precision=HIGH)]
    another operation x14 -> x0, local copies, waits for them, and re-layouts: 9.42 us -> none  [the longest x8 6.06 us: mix_left(): return jnp.stack([real, imag])]
    slice x5 -> x0, local copies, waits for them, and re-layouts: 6.85 us -> none  [the longest x2 4.46 us: mix_right(): values[0]]
    reshape x4 -> x0, local copies, waits for them, and re-layouts: 5.84 us -> none  [the longest x1 3.47 us: unpack_block(): return jnp.transpose(shaped, (0, 1, 2, 4, 3, 5)).reshape(2, -1)]
    eq x2 -> x0, other arithmetic: 2.48 us -> none  [select_gate(): pass_order[which] == jnp.arange(gate_bank.shape[0], dtype=jnp.int32)]
where the time goes in v1:
time: 102 us
  Pallas kernels  99.6 us (98%)
  local copies, waits for them, and re-layouts  2.61 us (3%)
    pallas_call x1, Pallas kernels, per_device(): pl.pallas_call(functools.partial(kernel, groups, wa_count, mid), out_shap...  99.6 us
    unnamed x1, local copies, waits for them, and re-layouts  2.61 us

profile of v1, /device:TPU:0, one launch (start us, length us, event | category | flops | bytes accessed | tf_op | source)
XLA Modules:
  0.0 102.2 jit_solution(1298098468888828550)
XLA Ops:
  0.0 99.6 %shard_map.37 = f32[8,16,2,2,8,128]{5,4,3,2,1,0:T(8,128)} custom-call(s32[4]{0:T(128)} %order_ref.1, f32[4,2,128,128]{3,2,1,0:T(8,128)} %bank_ref.1, f32[8,16,2,2,8,128]{5,4,3,2,1,0:T(8,128)} %bitcast.11), custom_call_target="tpu_custom_call" | custom-call | tf_op jit(solution)/shard_map/pallas_call | solution.py:168
  99.6 2.6 %copy.7 = f32[2,262144]{1,0:T(2,128)} copy(f32[2,262144]{1,0:T(2,128)} %bitcast.10) | data formatting | bytes 4194304

commit v2 on v1

--- a/solution.py
+++ b/solution.py
@@ -167,13 +167,13 @@
     slots = 4 * groups
     out = pl.pallas_call(
         functools.partial(kernel, groups, wa_count, mid),
-        out_shape=jax.ShapeDtypeStruct(shape, jnp.float32),
+        out_shape=pltpu.VMEM(shape, jnp.float32),
         in_specs=[
             pl.BlockSpec(memory_space=pltpu.SMEM),
             pl.BlockSpec(memory_space=pltpu.VMEM),
             pl.BlockSpec(memory_space=pl.ANY),
         ],
-        out_specs=pl.BlockSpec(memory_space=pl.ANY),
+        out_specs=pl.BlockSpec(memory_space=pltpu.VMEM),
         scratch_shapes=[
             pltpu.VMEM((2 * lanes, 2 * lanes), jnp.float32),
             pltpu.VMEM((4 * lanes, 4 * lanes), jnp.float32),

time: 102 us -> 101 us (level)
  local copies, waits for them, and re-layouts: 2.61 us -> 1.32 us
    unnamed x1, local copies, waits for them, and re-layouts: 2.61 us -> 1.32 us
where the time goes in v2:
time: 101 us
  Pallas kernels  99.5 us (99%)
  local copies, waits for them, and re-layouts  1.32 us (1%)
    pallas_call x1, Pallas kernels, per_device(): pl.pallas_call(functools.partial(kernel, groups, wa_count, mid), out_shap...  99.5 us

profile of v2, /device:TPU:0, one launch (start us, length us, event | category | flops | bytes accessed | tf_op | source)
XLA Modules:
  0.0 100.8 jit_solution(16856362902485572324)
XLA Ops:
  0.0 99.5 %shard_map.37 = f32[8,16,2,2,8,128]{5,4,3,2,1,0:T(8,128)S(1)} custom-call(s32[4]{0:T(128)} %order_ref.1, f32[4,2,128,128]{3,2,1,0:T(8,128)} %bank_ref.1, f32[8,16,2,2,8,128]{5,4,3,2,1,0:T(8,128)} %bitcast.11), custom_call_target="tpu_custom_call" | custom-call | tf_op jit(solution)/shard_map/pallas_call | solution.py:168
  99.5 1.3 %copy.7 = f32[2,262144]{1,0:T(2,128)} copy(f32[2,262144]{1,0:T(2,128)S(1)} %bitcast.10) | data formatting | bytes 4194304

commit v3 on v2

--- a/solution.py
+++ b/solution.py
@@ -40,8 +40,8 @@
     return jnp.where(slot == ((w0 * groups + a) * 2 + high) * mid + m, 1.0, 0.0).astype(jnp.float32)
 
 
-def kernel(groups, wa_count, mid, order_ref, bank_ref, x_ref, out_ref, lanes_gate, rows_gate,
-           buf, obuf, fs, fr, bs, br, own):
+def kernel(groups, wa_count, mid, order_hbm, bank_hbm, x_ref, out_ref, order_ref, bank_ref,
+           lanes_gate, rows_gate, buf, obuf, fs, fr, bs, br, own, load, round_sem):
     gate_rows = bank_ref.shape[2]
     rows = 2 * gate_rows
     a = lax.axis_index("pb")
@@ -97,18 +97,34 @@
             send_sem=bs.at[c, slot(p)], recv_sem=br.at[c, slot(p)],
             device_id=device(p), device_id_type=MESH)
 
+    across = (a, (w2 + 1) % 2, w0)
+    steps = [(a, w2, (w0 + 1) % 2)]
+    stride = 1
+    while stride < groups:
+        steps.append((a + stride * (1 - 2 * ((a // stride) % 2)), w2, w0))
+        stride *= 2
+
     barrier = pltpu.get_barrier_semaphore()
-    for p in peers:
+    for p in [across] + steps:
         pl.semaphore_signal(barrier, inc=1, device_id=device(p), device_id_type=MESH)
-    pl.semaphore_wait(barrier, len(peers))
-
-    for c in range(CHUNKS):
-        for p in peers:
+    pl.semaphore_wait(barrier, 1 + len(steps))
+
+    forward(0, across).start()
+    for k, p in enumerate(steps):
+        pl.semaphore_signal(round_sem.at[k], inc=1, device_id=device(p), device_id_type=MESH)
+        pl.semaphore_wait(round_sem.at[k], 1)
+
+    for c in range(CHUNKS):
+        for p in peers[1 if c == 0 else 0:]:
             forward(c, p).start()
+    fetch = [pltpu.make_async_copy(order_hbm, order_ref, load.at[0]),
+             pltpu.make_async_copy(bank_hbm, bank_ref, load.at[1])]
     stay = [pltpu.make_async_copy(piece(x_ref, me, c), held(buf, c, mine), own.at[0, c])
             for c in range(CHUNKS)]
-    for copy in stay:
+    for copy in fetch + stay:
         copy.start()
+    for copy in fetch:
+        copy.wait()
 
     gates = [bank_ref[order_ref[k]] for k in range(4)]
     first = embed(gates[0][0], gates[0][1])
@@ -169,12 +185,14 @@
         functools.partial(kernel, groups, wa_count, mid),
         out_shape=pltpu.VMEM(shape, jnp.float32),
         in_specs=[
-            pl.BlockSpec(memory_space=pltpu.SMEM),
-            pl.BlockSpec(memory_space=pltpu.VMEM),
+            pl.BlockSpec(memory_space=pl.ANY),
+            pl.BlockSpec(memory_space=pl.ANY),
             pl.BlockSpec(memory_space=pl.ANY),
         ],
         out_specs=pl.BlockSpec(memory_space=pltpu.VMEM),
         scratch_shapes=[
+            pltpu.SMEM(pass_order.shape, jnp.int32),
+            pltpu.VMEM(gate_bank.shape, jnp.float32),
             pltpu.VMEM((2 * lanes, 2 * lanes), jnp.float32),
             pltpu.VMEM((4 * lanes, 4 * lanes), jnp.float32),
             pltpu.VMEM((CHUNKS, 2 * lanes, SUB, lanes), jnp.float32),
@@ -184,6 +202,8 @@
             pltpu.SemaphoreType.DMA((CHUNKS, slots)),
             pltpu.SemaphoreType.DMA((CHUNKS, slots)),
             pltpu.SemaphoreType.DMA((2, CHUNKS)),
+            pltpu.SemaphoreType.DMA((2,)),
+            pltpu.SemaphoreType.REGULAR((groups.bit_length(),)),
         ],
         compiler_params=pltpu.CompilerParams(collective_id=0, has_side_effects=True),
     )(pass_order, gate_bank, x)

time: 101 us -> 99.9 us (0.989)
  Pallas kernels: 99.5 us -> 98.4 us
    pallas_call x1, Pallas kernels: 99.5 us -> 98.4 us  [per_device(): pl.pallas_call(functools.partial(kernel, groups, wa_count, mid), out_shap...]
where the time goes in v3:
time: 99.9 us; the launch traced here: 99.7 us
  Pallas kernels  98.4 us (98%)
  local copies, waits for them, and re-layouts  1.32 us (1%)
    pallas_call x1, Pallas kernels, per_device(): pl.pallas_call(functools.partial(kernel, groups, wa_count, mid), out_shap...  98.4 us

profile of v3, /device:TPU:0, one launch (start us, length us, event | category | flops | bytes accessed | tf_op | source)
XLA Modules:
  0.0 99.7 jit_solution(464136285825282100)
XLA Ops:
  0.0 98.4 %shard_map.37 = f32[8,16,2,2,8,128]{5,4,3,2,1,0:T(8,128)S(1)} custom-call(s32[4]{0:T(128)} %order_hbm.1, f32[4,2,128,128]{3,2,1,0:T(8,128)} %bank_hbm.1, f32[8,16,2,2,8,128]{5,4,3,2,1,0:T(8,128)} %bitcast.11), custom_call_target="tpu_custom_call" | custom-call | tf_op jit(solution)/shard_map/pallas_call | solution.py:184
  98.4 1.3 %copy.7 = f32[2,262144]{1,0:T(2,128)} copy(f32[2,262144]{1,0:T(2,128)S(1)} %bitcast.10) | data formatting | bytes 4194304

commit v4 on v3

--- a/solution.py
+++ b/solution.py
@@ -109,13 +109,31 @@
         pl.semaphore_signal(barrier, inc=1, device_id=device(p), device_id_type=MESH)
     pl.semaphore_wait(barrier, 1 + len(steps))
 
-    forward(0, across).start()
+    ends = w2 == 2 * wm // half
+    far = peers[:2 * groups]
+    near = peers[2 * groups:]
+    marker = near[1]
+
+    @pl.when(jnp.logical_not(ends))
+    def _():
+        forward(0, across).start()
+
     for k, p in enumerate(steps):
         pl.semaphore_signal(round_sem.at[k], inc=1, device_id=device(p), device_id_type=MESH)
         pl.semaphore_wait(round_sem.at[k], 1)
 
-    for c in range(CHUNKS):
-        for p in peers[1 if c == 0 else 0:]:
+    for p in near:
+        forward(0, p).start()
+
+    @pl.when(ends)
+    def _():
+        forward(0, marker).wait_send()
+        forward(0, across).start()
+
+    for p in far[1:]:
+        forward(0, p).start()
+    for c in range(1, CHUNKS):
+        for p in peers:
             forward(c, p).start()
     fetch = [pltpu.make_async_copy(order_hbm, order_ref, load.at[0]),
              pltpu.make_async_copy(bank_hbm, bank_ref, load.at[1])]
@@ -170,8 +188,13 @@
         pltpu.make_async_copy(held(obuf, c, mine), piece(out_ref, me, c), own.at[1, c]).wait()
     for c in range(CHUNKS):
         for p in peers:
-            forward(c, p).wait_send()
+            if c or p is not marker:
+                forward(c, p).wait_send()
             back(c, p).wait_send()
+
+    @pl.when(jnp.logical_not(ends))
+    def _():
+        forward(0, marker).wait_send()
 
 
 def per_device(groups, wa_count, state, gate_bank, pass_order):

time: 99.9 us -> 101 us (1.011)
  no operation moved by 1% of the time
where the time goes in v4:
time: 101 us
  Pallas kernels  99.2 us (98%)
  local copies, waits for them, and re-layouts  1.32 us (1%)
    pallas_call x1, Pallas kernels, per_device(): pl.pallas_call(functools.partial(kernel, groups, wa_count, mid), out_shap...  99.2 us

profile of v4, /device:TPU:0, one launch (start us, length us, event | category | flops | bytes accessed | tf_op | source)
XLA Modules:
  0.0 100.5 jit_solution(13257609943861396631)
XLA Ops:
  0.0 99.2 %shard_map.37 = f32[8,16,2,2,8,128]{5,4,3,2,1,0:T(8,128)S(1)} custom-call(s32[4]{0:T(128)} %order_hbm.1, f32[4,2,128,128]{3,2,1,0:T(8,128)} %bank_hbm.1, f32[8,16,2,2,8,128]{5,4,3,2,1,0:T(8,128)} %bitcast.11), custom_call_target="tpu_custom_call" | custom-call | tf_op jit(solution)/shard_map/pallas_call | solution.py:207
  99.2 1.3 %copy.7 = f32[2,262144]{1,0:T(2,128)} copy(f32[2,262144]{1,0:T(2,128)S(1)} %bitcast.10) | data formatting | bytes 4194304

commit v5 on v3

--- a/solution.py
+++ b/solution.py
@@ -103,6 +103,9 @@
     while stride < groups:
         steps.append((a + stride * (1 - 2 * ((a // stride) % 2)), w2, w0))
         stride *= 2
+
+    ends = w2 == 2 * wm // half
+    far = peers[:2 * groups]
 
     barrier = pltpu.get_barrier_semaphore()
     for p in [across] + steps:
@@ -160,6 +163,12 @@
             done = dot(rows_gate[...], tall)
             flat_out[pl.ds(2 * q, rows, SUB), :] = done[:rows]
             flat_out[pl.ds(2 * q + 1, rows, SUB), :] = done[rows:]
+        if c:
+            @pl.when(ends)
+            def _():
+                for p in far:
+                    back(c - 1, p).wait_send()
+
         for p in peers:
             back(c, p).start()
         pltpu.make_async_copy(held(obuf, c, mine), piece(out_ref, me, c), own.at[1, c]).start()
@@ -171,7 +180,14 @@
     for c in range(CHUNKS):
         for p in peers:
             forward(c, p).wait_send()
+        for p in peers[2 * groups if c + 1 < CHUNKS else 0:]:
             back(c, p).wait_send()
+
+    @pl.when(jnp.logical_not(ends))
+    def _():
+        for c in range(CHUNKS - 1):
+            for p in far:
+                back(c, p).wait_send()
 
 
 def per_device(groups, wa_count, state, gate_bank, pass_order):

time: 99.9 us -> 99.8 us (level)
  no operation moved by 1% of the time
where the time goes in v5:
time: 99.8 us; the launch traced here: 99.7 us
  Pallas kernels  98.4 us (99%)
  local copies, waits for them, and re-layouts  1.32 us (1%)
    pallas_call x1, Pallas kernels, per_device(): pl.pallas_call(functools.partial(kernel, groups, wa_count, mid), out_shap...  98.4 us

profile of v5, /device:TPU:0, one launch (start us, length us, event | category | flops | bytes accessed | tf_op | source)
XLA Modules:
  0.0 99.7 jit_solution(10452034485915083075)
XLA Ops:
  0.0 98.4 %shard_map.37 = f32[8,16,2,2,8,128]{5,4,3,2,1,0:T(8,128)S(1)} custom-call(s32[4]{0:T(128)} %order_hbm.1, f32[4,2,128,128]{3,2,1,0:T(8,128)} %bank_hbm.1, f32[8,16,2,2,8,128]{5,4,3,2,1,0:T(8,128)} %bitcast.11), custom_call_target="tpu_custom_call" | custom-call | tf_op jit(solution)/shard_map/pallas_call | solution.py:200
  98.4 1.3 %copy.7 = f32[2,262144]{1,0:T(2,128)} copy(f32[2,262144]{1,0:T(2,128)S(1)} %bitcast.10) | data formatting | bytes 4194304

commit v6 on v3

--- a/solution.py
+++ b/solution.py
@@ -160,7 +160,7 @@
             done = dot(rows_gate[...], tall)
             flat_out[pl.ds(2 * q, rows, SUB), :] = done[:rows]
             flat_out[pl.ds(2 * q + 1, rows, SUB), :] = done[rows:]
-        for p in peers:
+        for p in peers if c + 1 < CHUNKS else peers[::-1]:
             back(c, p).start()
         pltpu.make_async_copy(held(obuf, c, mine), piece(out_ref, me, c), own.at[1, c]).start()
 

time: 99.9 us -> 99.3 us (level)
  no operation moved by 1% of the time
where the time goes in v6:
time: 99.3 us; the launch traced here: 99.2 us
  Pallas kernels  97.8 us (98%)
  local copies, waits for them, and re-layouts  1.32 us (1%)
    pallas_call x1, Pallas kernels, per_device(): pl.pallas_call(functools.partial(kernel, groups, wa_count, mid), out_shap...  97.8 us

profile of v6, /device:TPU:0, one launch (start us, length us, event | category | flops | bytes accessed | tf_op | source)
XLA Modules:
  0.0 99.2 jit_solution(11206720617963500587)
XLA Ops:
  0.0 97.8 %shard_map.37 = f32[8,16,2,2,8,128]{5,4,3,2,1,0:T(8,128)S(1)} custom-call(s32[4]{0:T(128)} %order_hbm.1, f32[4,2,128,128]{3,2,1,0:T(8,128)} %bank_hbm.1, f32[8,16,2,2,8,128]{5,4,3,2,1,0:T(8,128)} %bitcast.11), custom_call_target="tpu_custom_call" | custom-call | tf_op jit(solution)/shard_map/pallas_call | solution.py:184
  97.8 1.3 %copy.7 = f32[2,262144]{1,0:T(2,128)} copy(f32[2,262144]{1,0:T(2,128)S(1)} %bitcast.10) | data formatting | bytes 4194304

commit v7 on v6

--- a/solution.py
+++ b/solution.py
@@ -109,13 +109,14 @@
         pl.semaphore_signal(barrier, inc=1, device_id=device(p), device_id_type=MESH)
     pl.semaphore_wait(barrier, 1 + len(steps))
 
-    forward(0, across).start()
+    for c in range(CHUNKS):
+        forward(c, across).start()
     for k, p in enumerate(steps):
         pl.semaphore_signal(round_sem.at[k], inc=1, device_id=device(p), device_id_type=MESH)
         pl.semaphore_wait(round_sem.at[k], 1)
 
     for c in range(CHUNKS):
-        for p in peers[1 if c == 0 else 0:]:
+        for p in peers[1:]:
             forward(c, p).start()
     fetch = [pltpu.make_async_copy(order_hbm, order_ref, load.at[0]),
              pltpu.make_async_copy(bank_hbm, bank_ref, load.at[1])]

time: 99.3 us -> 99.1 us (level)
  no operation moved by 1% of the time
where the time goes in v7:
time: 99.1 us; the launch traced here: 99 us
  Pallas kernels  97.6 us (98%)
  local copies, waits for them, and re-layouts  1.32 us (1%)
    pallas_call x1, Pallas kernels, per_device(): pl.pallas_call(functools.partial(kernel, groups, wa_count, mid), out_shap...  97.6 us

profile of v7, /device:TPU:0, one launch (start us, length us, event | category | flops | bytes accessed | tf_op | source)
XLA Modules:
  0.0 99.0 jit_solution(9635287195828059481)
XLA Ops:
  0.0 97.6 %shard_map.37 = f32[8,16,2,2,8,128]{5,4,3,2,1,0:T(8,128)S(1)} custom-call(s32[4]{0:T(128)} %order_hbm.1, f32[4,2,128,128]{3,2,1,0:T(8,128)} %bank_hbm.1, f32[8,16,2,2,8,128]{5,4,3,2,1,0:T(8,128)} %bitcast.11), custom_call_target="tpu_custom_call" | custom-call | tf_op jit(solution)/shard_map/pallas_call | solution.py:185
  97.7 1.3 %copy.7 = f32[2,262144]{1,0:T(2,128)} copy(f32[2,262144]{1,0:T(2,128)S(1)} %bitcast.10) | data formatting | bytes 4194304
